TPU v7x, 256 devices: a whole 4x4x8 slice. The times are simulated.
256 devices in a mesh: cfg: 2 (over core), blk: 4 (over y), uly: 32 (over x, z).
Axes of the slice: x: 4, y: 4, z: 8, core: 2. Of those that a mesh axis runs over, the one named last changes fastest.
Arguments:
- queries: bfloat16 [16384, 4096], P(('cfg', 'blk', 'uly')), parts along dimension 0, may hold values from -24 to 24
- key_states: bfloat16 [16384, 4096], P(('cfg', 'blk', 'uly')), parts along dimension 0, may hold values from -24 to 24
- value_states: bfloat16 [16384, 4096], P(('cfg', 'blk', 'uly')), parts along dimension 0, may hold values from -6 to 6
- tile_list: int32 [16, 12], replicated, may hold values from 0 to 15, as said below
- tile_used: int32 [16], replicated, may hold values from 1 to 12, as said below
Outputs:
- attended: bfloat16 [16384, 4096], P(('cfg', 'blk', 'uly')), parts along dimension 0
There are 2 independent parts, one for each index of `cfg`. A program takes and returns all parts, laid end to end along the dimension named above; an argument that names none is the same for every part. Nothing has to cross between parts.
Inputs may be any that keep to these rules, and one draw needn't show every extreme that they name: `tile_list`: tiles are numbered with the temporal tile row slowest, then 2 rows along the height, then 2 along the width. The first tile_used[i] entries of row i are distinct tiles whose temporal tile row differs from that of tile i by at most one, and the first of them is tile i itself; the other entries of the row are to be ignored. `tile_used`: in every draw some tile lists all 12 tiles of its window and some tile lists only itself.
All inputs are finite; a program needn't handle non-finite values.
Results may differ from a plain program's by a relative error of at most 0.0047.
Values may be sent and summed in bfloat16 or wider, within the bound.
No kernel may reach another device: no remote copies, remote signals or barrier semaphores. Data moves between devices by JAX's collectives and lax.ppermute only.
A program may use at most 64 MiB of HBM per device.

v0:
```python
import math

import jax
import jax.numpy as jnp
from jax import lax
from jax.experimental import pallas as pl
from jax.experimental.pallas import tpu as pltpu
from jax.sharding import PartitionSpec as P

HD = 128
TILE = 512
TILES_HERE = 4
SPAN = 12
LONG = 8
STEP = 4
SLOTS = 36
LOG2_SCALE = HD ** -0.5 * math.log2(math.e)


def plan_kernel(tile_list, tile_used, blk, key_tile, row_tile, trips):
    first = blk[0] * TILES_HERE
    total = tile_used[first]
    for i in range(1, TILES_HERE):
        total = total + tile_used[first + i]
    split = total > SLOTS

    def add(i, group, filled):
        def put(s, filled):
            key_tile[group, filled] = tile_list[first + i, s] - first + TILES_HERE
            row_tile[group, filled] = jnp.int32(i)
            return filled + 1

        return lax.fori_loop(0, tile_used[first + i], put, filled)

    def close(group, filled):
        for j in range(STEP - 1):
            key_tile[group, filled + j] = jnp.int32(TILES_HERE)
            row_tile[group, filled + j] = jnp.int32(TILES_HERE)
        trips[group] = filled // LONG
        trips[3 + group] = (lax.rem(filled, LONG) + (STEP - 1)) // STEP

    filled = jnp.int32(0)
    for i in range(TILES_HERE - 1):
        filled = add(i, 0, filled)
    last_group = split.astype(jnp.int32)
    start = jnp.where(split, 0, filled)
    close(0, filled)
    trips[1] = jnp.int32(0)
    trips[4] = jnp.int32(0)
    ended = add(TILES_HERE - 1, last_group, start)
    close(last_group, ended)
    trips[2] = last_group + 1


def plan(tile_list, tile_used, blk):
    smem = pl.BlockSpec(memory_space=pltpu.SMEM)
    width = SLOTS + STEP
    return pl.pallas_call(
        plan_kernel,
        in_specs=[smem] * 3,
        out_specs=[smem] * 3,
        out_shape=[
            jax.ShapeDtypeStruct((2, width), jnp.int32),
            jax.ShapeDtypeStruct((2, width), jnp.int32),
            jax.ShapeDtypeStruct((5,), jnp.int32),
        ],
    )(tile_list, tile_used, blk)


def attention_kernel(
    key_tile, row_tile, trips, q_in, low_in, own_in, high_in, out, q_all, kv, scores, tops, sums, sems
):
    near = (own_in, low_in, high_in)
    place = (1, 0, 2)
    third = kv.shape[1] // 3
    first_copies = [pltpu.make_async_copy(q_in, q_all, sems.at[0])]
    later_copies = []
    for j in range(3):
        span = pl.ds(third * place[j], third)
        first_copies.append(pltpu.make_async_copy(near[j].at[:, 0], kv.at[0, span], sems.at[1 + j]))
        later_copies.append(pltpu.make_async_copy(near[j].at[:, 1], kv.at[1, span], sems.at[4 + j]))
    for c in first_copies + later_copies:
        c.start()
    tops[...] = jnp.full(tops.shape, -3e38, jnp.float32)
    sums[...] = jnp.zeros_like(sums)
    for c in first_copies:
        c.wait()

    def walk(g, work):
        def long(c, _):
            work(c * LONG, LONG)
            return 0

        def short(c, _):
            work(trips[g] * LONG + c * STEP, STEP)
            return 0

        lax.fori_loop(0, trips[g], long, 0)
        lax.fori_loop(0, trips[3 + g], short, 0)

    def group(g, _):
        def score(s, count):
            for j in range(count):
                here = s + j
                row = row_tile[g, here]
                q = q_all[pl.ds(8 * jnp.minimum(row, TILES_HERE - 1), 8)].reshape(TILE, HD)
                k = kv[0, pl.ds(8 * key_tile[g, here], 8)].reshape(TILE, HD)
                dots = lax.dot_general(
                    q, k, (((1,), (1,)), ((), ())), preferred_element_type=jnp.float32
                )
                scores[here] = dots
                lanes = [dots[:, HD * n : HD * (n + 1)] for n in range(TILE // HD)]
                top = jnp.maximum(jnp.maximum(lanes[0], lanes[1]), jnp.maximum(lanes[2], lanes[3]))
                tops[row] = jnp.maximum(tops[row], top)

        walk(g, score)

        @pl.when(g == 0)
        def _():
            for c in later_copies:
                c.wait()

        for i in range(TILES_HERE):
            top = jnp.max(tops[i], axis=1, keepdims=True) * LOG2_SCALE
            tops[i] = jnp.broadcast_to(top, (TILE, HD))

        def weigh(s, count):
            for j in range(count):
                here = s + j
                row = row_tile[g, here]
                v = kv[1, pl.ds(8 * key_tile[g, here], 8)].reshape(TILE, HD)
                v = jnp.concatenate([v, jnp.ones_like(v)], axis=1)
                top = tops[row]
                weights = [
                    jnp.exp2(scores[here, :, HD * n : HD * (n + 1)] * LOG2_SCALE - top)
                    for n in range(TILE // HD)
                ]
                weights = jnp.concatenate([w.astype(jnp.bfloat16) for w in weights], axis=1)
                sums[row] += jnp.dot(weights, v, preferred_element_type=jnp.float32)

        walk(g, weigh)
        return 0

    lax.fori_loop(0, trips[2], group, 0)
    for i in range(TILES_HERE):
        result = sums[i, :, :HD] / sums[i, :, HD:]
        out[pl.ds(8 * i, 8)] = result.astype(jnp.bfloat16).reshape(8, TILE // 8, HD)


def attend(planned, q, low, own, high):
    anywhere = pl.BlockSpec(memory_space=pl.ANY)
    return pl.pallas_call(
        attention_kernel,
        grid_spec=pltpu.PrefetchScalarGridSpec(
            num_scalar_prefetch=3,
            grid=(1,),
            in_specs=[anywhere] * 4,
            out_specs=pl.BlockSpec(q.shape, lambda i, *_: (0, 0, 0)),
            scratch_shapes=[
                pltpu.VMEM(q.shape, q.dtype),
                pltpu.VMEM((2, 3 * q.shape[0]) + q.shape[1:], q.dtype),
                pltpu.VMEM((SLOTS, TILE, TILE), jnp.float32),
                pltpu.VMEM((TILES_HERE + 1, TILE, HD), jnp.float32),
                pltpu.VMEM((TILES_HERE + 1, TILE, 2 * HD), jnp.float32),
                pltpu.SemaphoreType.DMA((7,)),
            ],
        ),
        out_shape=jax.ShapeDtypeStruct(q.shape, q.dtype),
        compiler_params=pltpu.CompilerParams(vmem_limit_bytes=49 * 2**20),
        cost_estimate=pl.CostEstimate(
            flops=32 * 4 * TILE * TILE * HD, bytes_accessed=4 * 2**20, transcendentals=32 * TILE * TILE
        ),
    )(*planned, q, low, own, high)


def pack_kernel(*refs):
    out = refs[-1]
    ins = refs[:out.shape[1]] if len(out.shape) == 4 else refs[:1]
    for h in range(out.shape[0]):
        for a, r in enumerate(ins):
            piece = r[:, HD * h : HD * (h + 1)]
            if len(ins) > 1:
                out[h, a] = piece
            else:
                out[h] = piece


def pack(*arrays, after=None):
    rows, width = arrays[0].shape
    heads = width // HD
    steps = 2
    inner = (len(arrays), rows, HD) if len(arrays) > 1 else (rows, HD)
    nbytes = 2 * len(arrays) * rows * width * 2
    return pl.pallas_call(
        pack_kernel,
        grid=(steps,),
        in_specs=[pl.BlockSpec((rows, width // steps), lambda i: (0, i))] * len(arrays)
        + [pl.BlockSpec(memory_space=pltpu.VMEM)] * (after is not None),
        out_specs=pl.BlockSpec((heads // steps,) + inner, lambda i: (i,) + (0,) * len(inner)),
        out_shape=jax.ShapeDtypeStruct((heads,) + inner, arrays[0].dtype),
        cost_estimate=pl.CostEstimate(flops=0, bytes_accessed=nbytes, transcendentals=0),
    )(*arrays, *([] if after is None else [after]))


def second_cores_turn(token, along):
    uly = lax.axis_size("uly")
    half = lax.axis_size("blk") * uly
    apart = half // 2 + uly // 2 + along // 2
    pairs = [(half + i, half + (i ^ apart)) for i in range(half)]
    return lax.ppermute(token, ("cfg", "blk", "uly"), pairs)


def exchange(x):
    return lax.all_to_all(x, "uly", split_axis=0, concat_axis=0, tiled=True)


def body(queries, key_states, value_states, tile_list, tile_used):
    blk = lax.axis_index("blk").astype(jnp.int32).reshape(1)
    count = lax.axis_size("blk")
    up = [(i, (i + 1) % count) for i in range(count)]
    down = [((i + 1) % count, i) for i in range(count)]
    turn = second_cores_turn(tile_used, TILE // queries.shape[0])
    kv = exchange(pack(key_states, value_states, after=turn))
    q = pack(queries)
    planned = plan(tile_list, tile_used, blk)
    kv, q, planned = lax.optimization_barrier((kv, q, planned))
    low = lax.ppermute(kv, "blk", up)
    high = lax.ppermute(kv, "blk", down)
    q = exchange(q)
    out = attend(planned, q, low, kv, high)
    out = exchange(out)
    return jnp.transpose(out, (1, 0, 2)).reshape(queries.shape)


def solution(mesh):
    spec = P(("cfg", "blk", "uly"), None)
    return jax.shard_map(
        body,
        mesh=mesh,
        in_specs=(spec, spec, spec, P(), P()),
        out_specs=spec,
        check_vma=False,
    )
```

profile of v0, /device:TPU:49, one launch (start us, length us, event | category | flops | bytes accessed | tf_op | source)
XLA Modules:
  0.0 97.7 jit_solution(3814484168628365417)
XLA Ops:
  0.0 10.1 %collective-permute-start = (s32[16]{0:T(128)}, s32[16]{0:T(128)S(1)}, u32[]{:S(2)}, u32[]{:S(2)}) collective-permute-start(s32[16]{0:T(128)} %tile_used.1), channel_id=1, source_target_pairs={{128,212},{129,213},{130,214},{131,215},{132,208},{133,209},{134,2... | collective-permute-start | bytes 200 | tf_op jit(solution)/shard_map/ppermute | solution.py:210
  10.1 3.0 %collective-permute-done.refs_2_ = s32[16]{0:T(128)S(1)} collective-permute-done((s32[16]{0:T(128)}, s32[16]{0:T(128)S(1)}, u32[]{:S(2)}, u32[]{:S(2)}) %collective-permute-start) | collective-permute-done | bytes 96 | tf_op jit(solution)/shard_map/ppermute | solution.py:210
  13.1 0.0 copy-start.3
  13.1 0.5 copy-done.3
  13.6 2.1 %shard_map.55 = bf16[32,2,64,128]{3,2,1,0:T(8,128)(2,1)} custom-call(bf16[64,4096]{1,0:T(8,128)(2,1)} %refs_0_.2, bf16[64,4096]{1,0:T(8,128)(2,1)} %refs_1_.1, s32[16]{0:T(128)} %copy-done.3), custom_call_target="tpu_custom_call" | custom-call | bytes 2097152 | tf_op jit(solution)/shard_map/pallas_call | solution.py:194
  15.7 10.6 %all-to-all-start = ((bf16[32,2,64,128]{3,2,1,0:T(8,128)(2,1)}), bf16[32,2,64,128]{3,2,1,0:T(8,128)(2,1)S(1)}, u32[]{:S(2)}, u32[]{:S(2)}) async-start(bf16[32,2,64,128]{3,2,1,0:T(8,128)(2,1)} %shard_map.55), calls=%async_computation | async-start | bytes 2097152 | tf_op jit(solution)/shard_map/all_to_all | solution.py:214
  26.4 1.8 %shard_map.56 = bf16[32,64,128]{2,1,0:T(8,128)(2,1)} custom-call(bf16[64,4096]{1,0:T(8,128)(2,1)} %refs_0_.3), custom_call_target="tpu_custom_call" | custom-call | bytes 1048576 | tf_op jit(solution)/shard_map/pallas_call | solution.py:194
  28.2 1.8 %shard_map.57 = (s32[2,40]{1,0:T(2,128)}, s32[2,40]{1,0:T(2,128)}, s32[5]{0:T(128)}) custom-call(s32[16,12]{1,0:T(8,128)} %tile_list.1, s32[16]{0:T(128)} %tile_used.1, s32[1]{0:T(128)} %bitcast.blk), custom_call_target="tpu_custom_call" | custom-call | tf_op jit(solution)/shard_map/pallas_call | solution.py:58
  29.9 15.2 %all-to-all-done.own_in = bf16[32,2,64,128]{3,2,1,0:T(8,128)(2,1)S(1)} async-done(((bf16[32,2,64,128]{3,2,1,0:T(8,128)(2,1)}), bf16[32,2,64,128]{3,2,1,0:T(8,128)(2,1)S(1)}, u32[]{:S(2)}, u32[]{:S(2)}) %all-to-all-start) | async-done | bytes 1048608 | tf_op jit(solution)/shard_map/all_to_all | solution.py:214
  45.1 0.0 copy-start
  45.1 0.0 copy-start.1
  45.1 0.0 copy-start.2
  45.1 0.2 collective-permute-start.2
  45.3 1.3 %collective-permute-start.1 = (bf16[32,2,64,128]{3,2,1,0:T(8,128)(2,1)S(1)}, bf16[32,2,64,128]{3,2,1,0:T(8,128)(2,1)S(1)}, u32[]{:S(2)}, u32[]{:S(2)}) collective-permute-start(bf16[32,2,64,128]{3,2,1,0:T(8,128)(2,1)S(1)} %all-to-all-done.own_in), channel_id=1, source_target_pairs={{0,32},{32,64},{64,96},{96,0},{1,33},{33,65},{65,97},{97,1},{2,34}... | collective-permute-start | bytes 3145736 | tf_op jit(solution)/shard_map/ppermute | solution.py:227
  46.6 16.8 %all_to_all.15.q_in = bf16[32,64,128]{2,1,0:T(8,128)(2,1)S(1)} all-to-all(bf16[32,64,128]{2,1,0:T(8,128)(2,1)} %shard_map.56), channel_id=1, replica_groups=mesh['cfg'=2,'blk'=4,'uly'=32] {'uly'}, dimensions={0} | all-to-all | bytes 1048576 | tf_op jit(solution)/shard_map/all_to_all | solution.py:214
  63.4 0.0 collective-permute-done.2.high_in
  63.4 0.0 collective-permute-done.1.low_in
  63.4 0.0 copy-done
  63.4 0.0 copy-done.1
  63.5 0.0 copy-done.2
  63.5 16.3 %shard_map.58 = bf16[32,64,128]{2,1,0:T(8,128)(2,1)S(1)} custom-call(s32[2,40]{1,0:T(2,128)S(1)} %copy-done, s32[2,40]{1,0:T(2,128)S(1)} %copy-done.1, s32[5]{0:T(128)S(1)} %copy-done.2, bf16[32,64,128]{2,1,0:T(8,128)(2,1)S(1)} %all_to_all.15.q_in, bf16[32,2,64,128]{3,2,1,0:T(8,128)(2,1)S(1)} %collective-permute-done.1.low_in, ...), custom_call_target="tpu_custom_call" | custom-call | flops 4294967296 | bytes 4194304 | tf_op jit(solution)/shard_map/pallas_call | solution.py:152
  79.7 17.1 %all_to_all.16 = bf16[32,64,128]{2,1,0:T(8,128)(2,1)S(1)} all-to-all(bf16[32,64,128]{2,1,0:T(8,128)(2,1)S(1)} %shard_map.58), channel_id=1, replica_groups=mesh['cfg'=2,'blk'=4,'uly'=32] {'uly'}, dimensions={0} | all-to-all | bytes 1048576 | tf_op jit(solution)/shard_map/all_to_all | solution.py:214
  96.9 0.9 copy_bitcast_fusion
Async XLA Ops:
  0.0 13.1 %collective-permute-start = (s32[16]{0:T(128)}, s32[16]{0:T(128)S(1)}, u32[]{:S(2)}, u32[]{:S(2)}) collective-permute-start(s32[16]{0:T(128)} %tile_used.1), channel_id=1, source_target_pairs={{128,212},{129,213},{130,214},{131,215},{132,208},{133,209},{134,2... | collective-permute-start | bytes 200 | tf_op jit(solution)/shard_map/ppermute | solution.py:210
  13.1 0.5 copy-start.3
  15.7 29.4 %all-to-all-start = ((bf16[32,2,64,128]{3,2,1,0:T(8,128)(2,1)}), bf16[32,2,64,128]{3,2,1,0:T(8,128)(2,1)S(1)}, u32[]{:S(2)}, u32[]{:S(2)}) async-start(bf16[32,2,64,128]{3,2,1,0:T(8,128)(2,1)} %shard_map.55), calls=%async_computation | async-start | bytes 2097152 | tf_op jit(solution)/shard_map/all_to_all | solution.py:214
  45.1 18.3 %copy-start = (s32[2,40]{1,0:T(2,128)S(1)}, s32[2,40]{1,0:T(2,128)}, u32[]{:S(2)}) copy-start(s32[2,40]{1,0:T(2,128)} %get-tuple-element.16.key_tile) | copy-start | bytes 964
  45.1 18.3 %copy-start.1 = (s32[2,40]{1,0:T(2,128)S(1)}, s32[2,40]{1,0:T(2,128)}, u32[]{:S(2)}) copy-start(s32[2,40]{1,0:T(2,128)} %get-tuple-element.17.row_tile) | copy-start | bytes 964
  45.1 18.3 %copy-start.2 = (s32[5]{0:T(128)S(1)}, s32[5]{0:T(128)}, u32[]{:S(2)}) copy-start(s32[5]{0:T(128)} %get-tuple-element.18.trips) | copy-start | bytes 64
  45.1 18.3 %collective-permute-start.2 = (bf16[32,2,64,128]{3,2,1,0:T(8,128)(2,1)S(1)}, bf16[32,2,64,128]{3,2,1,0:T(8,128)(2,1)S(1)}, u32[]{:S(2)}, u32[]{:S(2)}) collective-permute-start(bf16[32,2,64,128]{3,2,1,0:T(8,128)(2,1)S(1)} %all-to-all-done.own_in), channel_id=1, source_target_pairs={{32,0},{64,32},{96,64},{0,96},{33,1},{65,33},{97,65},{1,97},{34,2}... | collective-permute-start | bytes 3145736 | tf_op jit(solution)/shard_map/ppermute | solution.py:228
  45.3 18.1 %collective-permute-start.1 = (bf16[32,2,64,128]{3,2,1,0:T(8,128)(2,1)S(1)}, bf16[32,2,64,128]{3,2,1,0:T(8,128)(2,1)S(1)}, u32[]{:S(2)}, u32[]{:S(2)}) collective-permute-start(bf16[32,2,64,128]{3,2,1,0:T(8,128)(2,1)S(1)} %all-to-all-done.own_in), channel_id=1, source_target_pairs={{0,32},{32,64},{64,96},{96,0},{1,33},{33,65},{65,97},{97,1},{2,34}... | collective-permute-start | bytes 3145736 | tf_op jit(solution)/shard_map/ppermute | solution.py:227
where the time goes:
time: 98.1 us; the launch traced here: 97.7 us
  blocking collectives  34 us (35%)
  starting transfers between devices  22.2 us (23%)
  Pallas kernels  21.9 us (22%)
  waiting for transfers between devices  18.2 us (19%)
  local copies, waits for them, and re-layouts  1.38 us (1%)
    all_to_all x2, blocking collectives, exchange(): return lax.all_to_all(x, 'uly', split_axis=0, concat_axis=0, tiled=True)  34 us
    pallas_call x1, Pallas kernels, attend(): pl.pallas_call(attention_kernel, grid_spec=pltpu.PrefetchScalarGridSpec(n...  16.3 us
    all_to_all x1, waiting for transfers between devices, exchange(): return lax.all_to_all(x, 'uly', split_axis=0, concat_axis=0, tiled=True)  15.2 us
    all_to_all x1, starting transfers between devices, exchange(): return lax.all_to_all(x, 'uly', split_axis=0, concat_axis=0, tiled=True)  10.6 us
    ppermute x1, starting transfers between devices, second_cores_turn(): return lax.ppermute(token, ('cfg', 'blk', 'uly'), pairs)  10.1 us
    pallas_call x2, Pallas kernels, pack(): pl.pallas_call(pack_kernel, grid=(steps,), in_specs=[pl.BlockSpec((rows,...  3.88 us
    ppermute x1, waiting for transfers between devices, second_cores_turn(): return lax.ppermute(token, ('cfg', 'blk', 'uly'), pairs)  2.97 us
  transfers between devices with their start and end apart: 4, of which 2 were waited for; matrix products, arithmetic and copies ran while one was open for 0% of the time, Pallas kernels for 4%

commit v1 on v0

--- a/solution.py
+++ b/solution.py
@@ -17,7 +17,7 @@
 LOG2_SCALE = HD ** -0.5 * math.log2(math.e)
 
 
-def plan_kernel(tile_list, tile_used, blk, key_tile, row_tile, trips):
+def plan_kernel(tile_list, tile_used, blk, turn, key_tile, row_tile, trips):
     first = blk[0] * TILES_HERE
     total = tile_used[first]
     for i in range(1, TILES_HERE):
@@ -52,19 +52,19 @@
     trips[2] = last_group + 1
 
 
-def plan(tile_list, tile_used, blk):
+def plan(tile_list, tile_used, blk, turn):
     smem = pl.BlockSpec(memory_space=pltpu.SMEM)
     width = SLOTS + STEP
     return pl.pallas_call(
         plan_kernel,
-        in_specs=[smem] * 3,
+        in_specs=[smem] * 3 + [pl.BlockSpec(memory_space=pl.ANY)],
         out_specs=[smem] * 3,
         out_shape=[
             jax.ShapeDtypeStruct((2, width), jnp.int32),
             jax.ShapeDtypeStruct((2, width), jnp.int32),
             jax.ShapeDtypeStruct((5,), jnp.int32),
         ],
-    )(tile_list, tile_used, blk)
+    )(tile_list, tile_used, blk, turn)
 
 
 def attention_kernel(
@@ -174,8 +174,7 @@
 
 
 def pack_kernel(*refs):
-    out = refs[-1]
-    ins = refs[:out.shape[1]] if len(out.shape) == 4 else refs[:1]
+    ins, out = refs[:-1], refs[-1]
     for h in range(out.shape[0]):
         for a, r in enumerate(ins):
             piece = r[:, HD * h : HD * (h + 1)]
@@ -185,7 +184,7 @@
                 out[h] = piece
 
 
-def pack(*arrays, after=None):
+def pack(*arrays):
     rows, width = arrays[0].shape
     heads = width // HD
     steps = 2
@@ -194,12 +193,11 @@
     return pl.pallas_call(
         pack_kernel,
         grid=(steps,),
-        in_specs=[pl.BlockSpec((rows, width // steps), lambda i: (0, i))] * len(arrays)
-        + [pl.BlockSpec(memory_space=pltpu.VMEM)] * (after is not None),
+        in_specs=[pl.BlockSpec((rows, width // steps), lambda i: (0, i))] * len(arrays),
         out_specs=pl.BlockSpec((heads // steps,) + inner, lambda i: (i,) + (0,) * len(inner)),
         out_shape=jax.ShapeDtypeStruct((heads,) + inner, arrays[0].dtype),
         cost_estimate=pl.CostEstimate(flops=0, bytes_accessed=nbytes, transcendentals=0),
-    )(*arrays, *([] if after is None else [after]))
+    )(*arrays)
 
 
 def second_cores_turn(token, along):
@@ -220,9 +218,10 @@
     up = [(i, (i + 1) % count) for i in range(count)]
     down = [((i + 1) % count, i) for i in range(count)]
     turn = second_cores_turn(tile_used, TILE // queries.shape[0])
-    kv = exchange(pack(key_states, value_states, after=turn))
+    key_states, turn = lax.optimization_barrier((key_states, turn))
+    kv = exchange(pack(key_states, value_states))
     q = pack(queries)
-    planned = plan(tile_list, tile_used, blk)
+    planned = plan(tile_list, tile_used, blk, turn)
     kv, q, planned = lax.optimization_barrier((kv, q, planned))
     low = lax.ppermute(kv, "blk", up)
     high = lax.ppermute(kv, "blk", down)

time: 98.1 us -> 98.4 us (level)
  no operation moved by 1% of the time
where the time goes in v1:
time: 98.4 us; the launch traced here: 97.2 us
  blocking collectives  33.9 us (34%)
  starting transfers between devices  22.2 us (23%)
  Pallas kernels  21.9 us (22%)
  waiting for transfers between devices  18.2 us (18%)
    all_to_all x2, blocking collectives, exchange(): return lax.all_to_all(x, 'uly', split_axis=0, concat_axis=0, tiled=True)  33.9 us
    pallas_call x1, Pallas kernels, attend(): pl.pallas_call(attention_kernel, grid_spec=pltpu.PrefetchScalarGridSpec(n...  16.3 us
    all_to_all x1, waiting for transfers between devices, exchange(): return lax.all_to_all(x, 'uly', split_axis=0, concat_axis=0, tiled=True)  15.2 us
    all_to_all x1, starting transfers between devices, exchange(): return lax.all_to_all(x, 'uly', split_axis=0, concat_axis=0, tiled=True)  10.6 us
    ppermute x1, starting transfers between devices, second_cores_turn(): return lax.ppermute(token, ('cfg', 'blk', 'uly'), pairs)  10.1 us
    pallas_call x2, Pallas kernels, pack(): pl.pallas_call(pack_kernel, grid=(steps,), in_specs=[pl.BlockSpec((rows,...  3.88 us
    ppermute x1, waiting for transfers between devices, second_cores_turn(): return lax.ppermute(token, ('cfg', 'blk', 'uly'), pairs)  2.97 us
  transfers between devices with their start and end apart: 4, of which 2 were waited for; matrix products, arithmetic and copies ran while one was open for 0% of the time, Pallas kernels for 4%

profile of v1, /device:TPU:49, one launch (start us, length us, event | category | flops | bytes accessed | tf_op | source)
XLA Modules:
  0.0 97.2 jit_solution(7998202449442515640)
XLA Ops:
  0.0 10.1 %collective-permute-start = (s32[16]{0:T(128)}, s32[16]{0:T(128)S(1)}, u32[]{:S(2)}, u32[]{:S(2)}) collective-permute-start(s32[16]{0:T(128)} %tile_used.1), channel_id=1, source_target_pairs={{128,212},{129,213},{130,214},{131,215},{132,208},{133,209},{134,2... | collective-permute-start | bytes 200 | tf_op jit(solution)/shard_map/ppermute | solution.py:208
  10.1 3.0 %collective-permute-done.turn = s32[16]{0:T(128)S(1)} collective-permute-done((s32[16]{0:T(128)}, s32[16]{0:T(128)S(1)}, u32[]{:S(2)}, u32[]{:S(2)}) %collective-permute-start) | collective-permute-done | bytes 96 | tf_op jit(solution)/shard_map/ppermute | solution.py:208
  13.1 0.0 copy-start.3
  13.1 2.1 %shard_map.55 = bf16[32,2,64,128]{3,2,1,0:T(8,128)(2,1)} custom-call(bf16[64,4096]{1,0:T(8,128)(2,1)} %refs_0_.1, bf16[64,4096]{1,0:T(8,128)(2,1)} %refs_1_.1), custom_call_target="tpu_custom_call" | custom-call | bytes 2097152 | tf_op jit(solution)/shard_map/pallas_call | solution.py:193
  15.2 0.0 copy-done.3
  15.2 10.6 %all-to-all-start = ((bf16[32,2,64,128]{3,2,1,0:T(8,128)(2,1)}), bf16[32,2,64,128]{3,2,1,0:T(8,128)(2,1)S(1)}, u32[]{:S(2)}, u32[]{:S(2)}) async-start(bf16[32,2,64,128]{3,2,1,0:T(8,128)(2,1)} %shard_map.55), calls=%async_computation | async-start | bytes 2097152 | tf_op jit(solution)/shard_map/all_to_all | solution.py:212
  25.9 1.8 %shard_map.56 = bf16[32,64,128]{2,1,0:T(8,128)(2,1)} custom-call(bf16[64,4096]{1,0:T(8,128)(2,1)} %refs_0_.2), custom_call_target="tpu_custom_call" | custom-call | bytes 1048576 | tf_op jit(solution)/shard_map/pallas_call | solution.py:193
  27.7 1.7 %shard_map.57 = (s32[2,40]{1,0:T(2,128)}, s32[2,40]{1,0:T(2,128)}, s32[5]{0:T(128)}) custom-call(s32[16,12]{1,0:T(8,128)} %tile_list.1, s32[16]{0:T(128)} %tile_used.1, s32[1]{0:T(128)} %bitcast.blk, s32[16]{0:T(128)} %copy-done.3), custom_call_target="tpu_custom_call" | custom-call | tf_op jit(solution)/shard_map/pallas_call | solution.py:58
  29.4 15.2 %all-to-all-done.own_in = bf16[32,2,64,128]{3,2,1,0:T(8,128)(2,1)S(1)} async-done(((bf16[32,2,64,128]{3,2,1,0:T(8,128)(2,1)}), bf16[32,2,64,128]{3,2,1,0:T(8,128)(2,1)S(1)}, u32[]{:S(2)}, u32[]{:S(2)}) %all-to-all-start) | async-done | bytes 1048608 | tf_op jit(solution)/shard_map/all_to_all | solution.py:212
  44.6 0.0 copy-start
  44.6 0.0 copy-start.1
  44.6 0.0 copy-start.2
  44.6 0.2 collective-permute-start.2
  44.8 1.3 %collective-permute-start.1 = (bf16[32,2,64,128]{3,2,1,0:T(8,128)(2,1)S(1)}, bf16[32,2,64,128]{3,2,1,0:T(8,128)(2,1)S(1)}, u32[]{:S(2)}, u32[]{:S(2)}) collective-permute-start(bf16[32,2,64,128]{3,2,1,0:T(8,128)(2,1)S(1)} %all-to-all-done.own_in), channel_id=1, source_target_pairs={{0,32},{32,64},{64,96},{96,0},{1,33},{33,65},{65,97},{97,1},{2,34}... | collective-permute-start | bytes 3145736 | tf_op jit(solution)/shard_map/ppermute | solution.py:226
  46.1 16.8 %all_to_all.15.q_in = bf16[32,64,128]{2,1,0:T(8,128)(2,1)S(1)} all-to-all(bf16[32,64,128]{2,1,0:T(8,128)(2,1)} %shard_map.56), channel_id=1, replica_groups=mesh['cfg'=2,'blk'=4,'uly'=32] {'uly'}, dimensions={0} | all-to-all | bytes 1048576 | tf_op jit(solution)/shard_map/all_to_all | solution.py:212
  62.9 0.0 collective-permute-done.2.high_in
  62.9 0.0 collective-permute-done.1.low_in
  63.0 0.0 copy-done
  63.0 0.0 copy-done.1
  63.0 0.0 copy-done.2
  63.0 16.3 %shard_map.58 = bf16[32,64,128]{2,1,0:T(8,128)(2,1)S(1)} custom-call(s32[2,40]{1,0:T(2,128)S(1)} %copy-done, s32[2,40]{1,0:T(2,128)S(1)} %copy-done.1, s32[5]{0:T(128)S(1)} %copy-done.2, bf16[32,64,128]{2,1,0:T(8,128)(2,1)S(1)} %all_to_all.15.q_in, bf16[32,2,64,128]{3,2,1,0:T(8,128)(2,1)S(1)} %collective-permute-done.1.low_in, ...), custom_call_target="tpu_custom_call" | custom-call | flops 4294967296 | bytes 4194304 | tf_op jit(solution)/shard_map/pallas_call | solution.py:152
  79.3 17.1 %all_to_all.16 = bf16[32,64,128]{2,1,0:T(8,128)(2,1)S(1)} all-to-all(bf16[32,64,128]{2,1,0:T(8,128)(2,1)S(1)} %shard_map.58), channel_id=1, replica_groups=mesh['cfg'=2,'blk'=4,'uly'=32] {'uly'}, dimensions={0} | all-to-all | bytes 1048576 | tf_op jit(solution)/shard_map/all_to_all | solution.py:212
  96.4 0.9 copy_bitcast_fusion
Async XLA Ops:
  0.0 13.1 %collective-permute-start = (s32[16]{0:T(128)}, s32[16]{0:T(128)S(1)}, u32[]{:S(2)}, u32[]{:S(2)}) collective-permute-start(s32[16]{0:T(128)} %tile_used.1), channel_id=1, source_target_pairs={{128,212},{129,213},{130,214},{131,215},{132,208},{133,209},{134,2... | collective-permute-start | bytes 200 | tf_op jit(solution)/shard_map/ppermute | solution.py:208
  13.1 2.1 %copy-start.3 = (s32[16]{0:T(128)}, s32[16]{0:T(128)S(1)}, u32[]{:S(2)}) copy-start(s32[16]{0:T(128)S(1)} %collective-permute-done.turn) | copy-start | bytes 196
  15.2 29.4 %all-to-all-start = ((bf16[32,2,64,128]{3,2,1,0:T(8,128)(2,1)}), bf16[32,2,64,128]{3,2,1,0:T(8,128)(2,1)S(1)}, u32[]{:S(2)}, u32[]{:S(2)}) async-start(bf16[32,2,64,128]{3,2,1,0:T(8,128)(2,1)} %shard_map.55), calls=%async_computation | async-start | bytes 2097152 | tf_op jit(solution)/shard_map/all_to_all | solution.py:212
  44.6 18.3 %copy-start = (s32[2,40]{1,0:T(2,128)S(1)}, s32[2,40]{1,0:T(2,128)}, u32[]{:S(2)}) copy-start(s32[2,40]{1,0:T(2,128)} %get-tuple-element.20.key_tile) | copy-start | bytes 964
  44.6 18.3 %copy-start.1 = (s32[2,40]{1,0:T(2,128)S(1)}, s32[2,40]{1,0:T(2,128)}, u32[]{:S(2)}) copy-start(s32[2,40]{1,0:T(2,128)} %get-tuple-element.21.row_tile) | copy-start | bytes 964
  44.6 18.3 %copy-start.2 = (s32[5]{0:T(128)S(1)}, s32[5]{0:T(128)}, u32[]{:S(2)}) copy-start(s32[5]{0:T(128)} %get-tuple-element.22.trips) | copy-start | bytes 64
  44.6 18.3 %collective-permute-start.2 = (bf16[32,2,64,128]{3,2,1,0:T(8,128)(2,1)S(1)}, bf16[32,2,64,128]{3,2,1,0:T(8,128)(2,1)S(1)}, u32[]{:S(2)}, u32[]{:S(2)}) collective-permute-start(bf16[32,2,64,128]{3,2,1,0:T(8,128)(2,1)S(1)} %all-to-all-done.own_in), channel_id=1, source_target_pairs={{32,0},{64,32},{96,64},{0,96},{33,1},{65,33},{97,65},{1,97},{34,2}... | collective-permute-start | bytes 3145736 | tf_op jit(solution)/shard_map/ppermute | solution.py:227
  44.8 18.1 %collective-permute-start.1 = (bf16[32,2,64,128]{3,2,1,0:T(8,128)(2,1)S(1)}, bf16[32,2,64,128]{3,2,1,0:T(8,128)(2,1)S(1)}, u32[]{:S(2)}, u32[]{:S(2)}) collective-permute-start(bf16[32,2,64,128]{3,2,1,0:T(8,128)(2,1)S(1)} %all-to-all-done.own_in), channel_id=1, source_target_pairs={{0,32},{32,64},{64,96},{96,0},{1,33},{33,65},{65,97},{97,1},{2,34}... | collective-permute-start | bytes 3145736 | tf_op jit(solution)/shard_map/ppermute | solution.py:226

commit v2 on v1

--- a/solution.py
+++ b/solution.py
@@ -11,7 +11,7 @@
 TILE = 512
 TILES_HERE = 4
 SPAN = 12
-LONG = 8
+LONG = 12
 STEP = 4
 SLOTS = 36
 LOG2_SCALE = HD ** -0.5 * math.log2(math.e)

time: 98.4 us -> 94.8 us (0.963)
  the two profiles are of different devices: /device:TPU:49 before, /device:TPU:41 now
where the time goes in v2:
time: 94.8 us; the launch traced here: 93.8 us
  blocking collectives  34 us (36%)
  starting transfers between devices  24.2 us (26%)
  Pallas kernels  18.4 us (19%)
  waiting for transfers between devices  16.3 us (17%)
    all_to_all x2, blocking collectives, exchange(): return lax.all_to_all(x, 'uly', split_axis=0, concat_axis=0, tiled=True)  34 us
    all_to_all x1, waiting for transfers between devices, exchange(): return lax.all_to_all(x, 'uly', split_axis=0, concat_axis=0, tiled=True)  15.3 us
    pallas_call x1, Pallas kernels, attend(): pl.pallas_call(attention_kernel, grid_spec=pltpu.PrefetchScalarGridSpec(n...  12.8 us
    ppermute x1, starting transfers between devices, second_cores_turn(): return lax.ppermute(token, ('cfg', 'blk', 'uly'), pairs)  12.1 us
    all_to_all x1, starting transfers between devices, exchange(): return lax.all_to_all(x, 'uly', split_axis=0, concat_axis=0, tiled=True)  10.6 us
    pallas_call x2, Pallas kernels, pack(): pl.pallas_call(pack_kernel, grid=(steps,), in_specs=[pl.BlockSpec((rows,...  3.88 us
  transfers between devices with their start and end apart: 4, of which 2 were waited for; matrix products, arithmetic and copies ran while one was open for 0% of the time, Pallas kernels for 4%

profile of v2, /device:TPU:41, one launch (start us, length us, event | category | flops | bytes accessed | tf_op | source)
XLA Modules:
  0.0 93.8 jit_solution(6853611508244227514)
XLA Ops:
  0.0 12.1 %collective-permute-start = (s32[16]{0:T(128)}, s32[16]{0:T(128)S(1)}, u32[]{:S(2)}, u32[]{:S(2)}) collective-permute-start(s32[16]{0:T(128)} %tile_used.1), channel_id=1, source_target_pairs={{128,212},{129,213},{130,214},{131,215},{132,208},{133,209},{134,2... | collective-permute-start | bytes 200 | tf_op jit(solution)/shard_map/ppermute | solution.py:208
  12.1 1.0 %collective-permute-done.turn = s32[16]{0:T(128)S(1)} collective-permute-done((s32[16]{0:T(128)}, s32[16]{0:T(128)S(1)}, u32[]{:S(2)}, u32[]{:S(2)}) %collective-permute-start) | collective-permute-done | bytes 96 | tf_op jit(solution)/shard_map/ppermute | solution.py:208
  13.2 0.0 copy-start.3
  13.2 2.1 %shard_map.55 = bf16[32,2,64,128]{3,2,1,0:T(8,128)(2,1)} custom-call(bf16[64,4096]{1,0:T(8,128)(2,1)} %refs_0_.1, bf16[64,4096]{1,0:T(8,128)(2,1)} %refs_1_.1), custom_call_target="tpu_custom_call" | custom-call | bytes 2097152 | tf_op jit(solution)/shard_map/pallas_call | solution.py:193
  15.2 0.0 copy-done.3
  15.2 10.6 %all-to-all-start = ((bf16[32,2,64,128]{3,2,1,0:T(8,128)(2,1)}), bf16[32,2,64,128]{3,2,1,0:T(8,128)(2,1)S(1)}, u32[]{:S(2)}, u32[]{:S(2)}) async-start(bf16[32,2,64,128]{3,2,1,0:T(8,128)(2,1)} %shard_map.55), calls=%async_computation | async-start | bytes 2097152 | tf_op jit(solution)/shard_map/all_to_all | solution.py:212
  25.9 1.8 %shard_map.56 = bf16[32,64,128]{2,1,0:T(8,128)(2,1)} custom-call(bf16[64,4096]{1,0:T(8,128)(2,1)} %refs_0_.2), custom_call_target="tpu_custom_call" | custom-call | bytes 1048576 | tf_op jit(solution)/shard_map/pallas_call | solution.py:193
  27.7 1.7 %shard_map.57 = (s32[2,40]{1,0:T(2,128)}, s32[2,40]{1,0:T(2,128)}, s32[5]{0:T(128)}) custom-call(s32[16,12]{1,0:T(8,128)} %tile_list.1, s32[16]{0:T(128)} %tile_used.1, s32[1]{0:T(128)} %bitcast.blk, s32[16]{0:T(128)} %copy-done.3), custom_call_target="tpu_custom_call" | custom-call | tf_op jit(solution)/shard_map/pallas_call | solution.py:58
  29.4 15.3 %all-to-all-done.own_in = bf16[32,2,64,128]{3,2,1,0:T(8,128)(2,1)S(1)} async-done(((bf16[32,2,64,128]{3,2,1,0:T(8,128)(2,1)}), bf16[32,2,64,128]{3,2,1,0:T(8,128)(2,1)S(1)}, u32[]{:S(2)}, u32[]{:S(2)}) %all-to-all-start) | async-done | bytes 1048608 | tf_op jit(solution)/shard_map/all_to_all | solution.py:212
  44.6 0.0 copy-start
  44.6 0.0 copy-start.1
  44.6 0.0 copy-start.2
  44.6 0.2 collective-permute-start.2
  44.8 1.3 %collective-permute-start.1 = (bf16[32,2,64,128]{3,2,1,0:T(8,128)(2,1)S(1)}, bf16[32,2,64,128]{3,2,1,0:T(8,128)(2,1)S(1)}, u32[]{:S(2)}, u32[]{:S(2)}) collective-permute-start(bf16[32,2,64,128]{3,2,1,0:T(8,128)(2,1)S(1)} %all-to-all-done.own_in), channel_id=1, source_target_pairs={{0,32},{32,64},{64,96},{96,0},{1,33},{33,65},{65,97},{97,1},{2,34}... | collective-permute-start | bytes 3145736 | tf_op jit(solution)/shard_map/ppermute | solution.py:226
  46.1 16.8 %all_to_all.15.q_in = bf16[32,64,128]{2,1,0:T(8,128)(2,1)S(1)} all-to-all(bf16[32,64,128]{2,1,0:T(8,128)(2,1)} %shard_map.56), channel_id=1, replica_groups=mesh['cfg'=2,'blk'=4,'uly'=32] {'uly'}, dimensions={0} | all-to-all | bytes 1048576 | tf_op jit(solution)/shard_map/all_to_all | solution.py:212
  62.9 0.0 collective-permute-done.2.high_in
  62.9 0.0 collective-permute-done.1.low_in
  63.0 0.0 copy-done
  63.0 0.0 copy-done.1
  63.0 0.0 copy-done.2
  63.0 12.8 %shard_map.58 = bf16[32,64,128]{2,1,0:T(8,128)(2,1)S(1)} custom-call(s32[2,40]{1,0:T(2,128)S(1)} %copy-done, s32[2,40]{1,0:T(2,128)S(1)} %copy-done.1, s32[5]{0:T(128)S(1)} %copy-done.2, bf16[32,64,128]{2,1,0:T(8,128)(2,1)S(1)} %all_to_all.15.q_in, bf16[32,2,64,128]{3,2,1,0:T(8,128)(2,1)S(1)} %collective-permute-done.1.low_in, ...), custom_call_target="tpu_custom_call" | custom-call | flops 4294967296 | bytes 4194304 | tf_op jit(solution)/shard_map/pallas_call | solution.py:152
  75.8 17.1 %all_to_all.16 = bf16[32,64,128]{2,1,0:T(8,128)(2,1)S(1)} all-to-all(bf16[32,64,128]{2,1,0:T(8,128)(2,1)S(1)} %shard_map.58), channel_id=1, replica_groups=mesh['cfg'=2,'blk'=4,'uly'=32] {'uly'}, dimensions={0} | all-to-all | bytes 1048576 | tf_op jit(solution)/shard_map/all_to_all | solution.py:212
  92.9 0.9 copy_bitcast_fusion
Async XLA Ops:
  0.0 13.2 %collective-permute-start = (s32[16]{0:T(128)}, s32[16]{0:T(128)S(1)}, u32[]{:S(2)}, u32[]{:S(2)}) collective-permute-start(s32[16]{0:T(128)} %tile_used.1), channel_id=1, source_target_pairs={{128,212},{129,213},{130,214},{131,215},{132,208},{133,209},{134,2... | collective-permute-start | bytes 200 | tf_op jit(solution)/shard_map/ppermute | solution.py:208
  13.2 2.1 %copy-start.3 = (s32[16]{0:T(128)}, s32[16]{0:T(128)S(1)}, u32[]{:S(2)}) copy-start(s32[16]{0:T(128)S(1)} %collective-permute-done.turn) | copy-start | bytes 196
  15.2 29.4 %all-to-all-start = ((bf16[32,2,64,128]{3,2,1,0:T(8,128)(2,1)}), bf16[32,2,64,128]{3,2,1,0:T(8,128)(2,1)S(1)}, u32[]{:S(2)}, u32[]{:S(2)}) async-start(bf16[32,2,64,128]{3,2,1,0:T(8,128)(2,1)} %shard_map.55), calls=%async_computation | async-start | bytes 2097152 | tf_op jit(solution)/shard_map/all_to_all | solution.py:212
  44.6 18.3 %copy-start = (s32[2,40]{1,0:T(2,128)S(1)}, s32[2,40]{1,0:T(2,128)}, u32[]{:S(2)}) copy-start(s32[2,40]{1,0:T(2,128)} %get-tuple-element.20.key_tile) | copy-start | bytes 964
  44.6 18.3 %copy-start.1 = (s32[2,40]{1,0:T(2,128)S(1)}, s32[2,40]{1,0:T(2,128)}, u32[]{:S(2)}) copy-start(s32[2,40]{1,0:T(2,128)} %get-tuple-element.21.row_tile) | copy-start | bytes 964
  44.6 18.3 %copy-start.2 = (s32[5]{0:T(128)S(1)}, s32[5]{0:T(128)}, u32[]{:S(2)}) copy-start(s32[5]{0:T(128)} %get-tuple-element.22.trips) | copy-start | bytes 64
  44.6 18.3 %collective-permute-start.2 = (bf16[32,2,64,128]{3,2,1,0:T(8,128)(2,1)S(1)}, bf16[32,2,64,128]{3,2,1,0:T(8,128)(2,1)S(1)}, u32[]{:S(2)}, u32[]{:S(2)}) collective-permute-start(bf16[32,2,64,128]{3,2,1,0:T(8,128)(2,1)S(1)} %all-to-all-done.own_in), channel_id=1, source_target_pairs={{32,0},{64,32},{96,64},{0,96},{33,1},{65,33},{97,65},{1,97},{34,2}... | collective-permute-start | bytes 3145736 | tf_op jit(solution)/shard_map/ppermute | solution.py:227
  44.8 18.1 %collective-permute-start.1 = (bf16[32,2,64,128]{3,2,1,0:T(8,128)(2,1)S(1)}, bf16[32,2,64,128]{3,2,1,0:T(8,128)(2,1)S(1)}, u32[]{:S(2)}, u32[]{:S(2)}) collective-permute-start(bf16[32,2,64,128]{3,2,1,0:T(8,128)(2,1)S(1)} %all-to-all-done.own_in), channel_id=1, source_target_pairs={{0,32},{32,64},{64,96},{96,0},{1,33},{33,65},{65,97},{97,1},{2,34}... | collective-permute-start | bytes 3145736 | tf_op jit(solution)/shard_map/ppermute | solution.py:226
